TPU v7x, 32 devices: a whole 2x2x4 slice. The times are simulated.
32 devices in a mesh: layer: 2 (over core), latent: 16 (over z, y, x).
Axes of the slice: x: 2, y: 2, z: 4, core: 2. Of those that a mesh axis runs over, the one named last changes fastest.
Arguments:
- activations: bfloat16 [2, 512, 2048], P('layer', 'latent'), may hold values from -15 to 15
- enc_weight: bfloat16 [2, 2048, 16384], P('layer', None, 'latent'), may hold values from -0.09375 to 0.09375
- enc_bias: float32 [16384], P('latent'), may hold values from -3 to 3
- dec_weight: bfloat16 [2, 16384, 2048], P('layer', 'latent'), may hold values from -0.1796875 to 0.1796875
- dec_bias: float32 [2, 2048], P('layer'), may hold values from -3 to 3
- active_mask: int32 [512, 16384], P(None, 'latent'), may hold values 0 or 1
Outputs:
- grad_enc: bfloat16 [2, 2048, 16384], P('layer', None, 'latent')
- grad_dec: bfloat16 [2, 16384, 2048], P('layer', 'latent')
- loss_value: float32 [], replicated
All inputs are finite; a program needn't handle non-finite values. No bound on the sum of `active_mask` on one device may be relied on, other than what follows from the above.
Results may differ from a plain program's by a relative error of at most 0.0065.
Values may be sent and summed in bfloat16 or wider, within the bound.
A program may use at most 128 MiB of HBM per device.

v0:
```python
import jax
import jax.numpy as jnp
from jax import lax
from jax.sharding import PartitionSpec as P

sparsity_weight = 0.4


def per_device(activations, enc_weight, enc_bias, dec_weight, dec_bias, active_mask):
    local_rows = activations[0]
    encoder = enc_weight[0]
    decoder = dec_weight[0]
    token_all = lax.all_gather(local_rows, "latent", axis=0, tiled=True)
    layer_pre = jnp.dot(token_all, encoder, preferred_element_type=jnp.float32)
    dec_float = decoder.astype(jnp.float32)
    row_norm = jnp.sqrt(jnp.sum(dec_float * dec_float, axis=1) + 1e-06)
    preact, norm_sum = lax.psum((layer_pre, row_norm), "layer")
    preact = preact + enc_bias
    gating = active_mask.astype(jnp.float32)
    latent_code = preact * gating
    code_b = latent_code.astype(jnp.bfloat16)
    layer_index = lax.axis_index("layer")
    recon_share = (
        lax.psum_scatter(
            jnp.dot(code_b, decoder, preferred_element_type=jnp.float32),
            "latent",
            scatter_dimension=0,
            tiled=True,
        )
        + dec_bias[0]
    )
    error_share = recon_share - local_rows.astype(jnp.float32)
    square_part = 0.5 * jnp.sum(error_share * error_share)
    error_b = lax.all_gather(error_share.astype(jnp.bfloat16), "latent", axis=0, tiled=True)
    layer_grad = jnp.einsum("td,fd->tf", error_b, decoder, preferred_element_type=jnp.float32)
    code_grad = lax.psum(layer_grad, "layer") + sparsity_weight * norm_sum
    preact_grad = (code_grad * gating).astype(jnp.bfloat16)
    grad_enc = jnp.einsum(
        "td,tf->df", token_all, preact_grad, preferred_element_type=jnp.float32
    ).astype(jnp.bfloat16)
    code_total = jnp.sum(latent_code, axis=0)
    shrink = sparsity_weight * code_total[:, None] * dec_float / row_norm[:, None]
    grad_dec = (
        jnp.einsum("tf,td->fd", code_b, error_b, preferred_element_type=jnp.float32) + shrink
    ).astype(jnp.bfloat16)
    sparse_part = jnp.where(
        layer_index == 0, sparsity_weight * jnp.sum(latent_code * norm_sum), 0.0
    )
    loss_total = lax.psum(square_part + sparse_part, ("layer", "latent"))
    loss_value = loss_total / (active_mask.shape[0] * token_all.shape[1])
    return (grad_enc[None], grad_dec[None], loss_value)


def solution(mesh):
    placed = (
        P("layer", "latent", None),
        P("layer", None, "latent"),
        P("latent"),
        P("layer", "latent", None),
        P("layer", None),
        P(None, "latent"),
    )
    return jax.shard_map(
        per_device,
        mesh=mesh,
        in_specs=placed,
        out_specs=(P("layer", None, "latent"), P("layer", "latent", None), P()),
        check_vma=False,
    )
```

profile of v0, /device:TPU:0, one launch (start us, length us, event | category | flops | bytes accessed | tf_op | source)
XLA Modules:
  0.0 342.8 jit_solution(5819471263152638103)
XLA Ops:
  7.2 0.0 all-gather.6.cloned.1.call-start
  7.2 0.7 all-gather.6.cloned.1.call-update
  7.9 0.0 all-reduce.3.cloned.1.call-start
  7.9 65.9 %all-gather.6.cloned.1.call-done = bf16[1,512,2048]{2,1,0:T(8,128)(2,1)} async-done(((bf16[1,32,2048]{2,1,0:T(8,128)(2,1)}), bf16[1,512,2048]{2,1,0:T(8,128)(2,1)}) %all-gather.6.cloned.1.call-update) | async-done | bytes 2097168 | tf_op jit(solution)/shard_map/all_gather | solution.py:13
  73.9 6.5 %fusion.8 = f32[512,1024]{1,0:T(8,128)} fusion(bf16[1,2048,1024]{2,1,0:T(8,128)(2,1)} %param.7, bf16[1,512,2048]{2,1,0:T(8,128)(2,1)} %all-gather.6.cloned.1.call-done), kind=kOutput, calls=%fused_computation.10 | convolution fusion | flops 2147483648 | bytes 8388608 | tf_op jit(solution)/shard_map/dot_general | solution.py:14
  80.4 0.0 all-reduce.3.cloned.1.call-update
  80.4 0.0 copy-start.1
  80.4 0.0 copy-start.4
  80.4 0.0 reduce-scatter.2.cloned.1.call-start
  80.4 3.2 fusion
  83.7 2.5 psum.30
  86.2 14.5 %all-reduce.3.cloned.1.call-done = f32[512,1024]{1,0:T(8,128)} async-done(((f32[512,1024]{1,0:T(8,128)}), f32[512,1024]{1,0:T(8,128)}) %all-reduce.3.cloned.1.call-update) | async-done | bytes 2097168 | tf_op jit(solution)/shard_map/psum | solution.py:17
  100.6 0.0 copy-done.1
  100.6 0.0 copy-done.4
  100.6 0.0 copy-start
  100.6 2.9 multiply_reduce_fusion
  103.6 0.0 copy-done
  103.6 4.4 %fusion.6 = f32[512,2048]{1,0:T(8,128)} fusion(bf16[1,1024,2048]{2,1,0:T(8,128)(2,1)S(1)} %copy-done, bf16[512,1024]{1,0:T(8,128)(2,1)S(1)} %get-tuple-element.8), kind=kOutput, calls=%fused_computation.8 | convolution fusion | flops 2147483648 | bytes 9437184 | tf_op jit(solution)/shard_map/dot_general | solution.py:25
  107.9 0.0 copy-start.2
  107.9 0.0 copy-start.3
  107.9 0.0 reduce-scatter.2.cloned.1.call-update
  108.0 0.0 all-gather.4.cloned.1.call-start
  108.0 96.5 %reduce-scatter.2.cloned.1.call-done = f32[32,2048]{1,0:T(8,128)} async-done(((f32[512,2048]{1,0:T(8,128)}), f32[32,2048]{1,0:T(8,128)}) %reduce-scatter.2.cloned.1.call-update) | async-done | bytes 262160 | tf_op jit(solution)/shard_map/reduce_scatter | solution.py:24
  204.5 0.0 copy-done.2
  204.5 0.0 copy-done.3
  204.5 2.3 multiply_reduce_fusion.1
  206.8 0.0 all-gather.4.cloned.1.call-update
  206.8 0.0 all-reduce.5.cloned.1.call-start
  206.9 60.8 %all-gather.4.cloned.1.call-done = bf16[512,2048]{1,0:T(8,128)(2,1)} async-done(((bf16[32,2048]{1,0:T(8,128)(2,1)}), bf16[512,2048]{1,0:T(8,128)(2,1)}) %all-gather.4.cloned.1.call-update) | async-done | bytes 2097168 | tf_op jit(solution)/shard_map/all_gather | solution.py:34
  267.7 6.5 %fusion.4 = f32[512,1024]{1,0:T(8,128)} fusion(bf16[512,2048]{1,0:T(8,128)(2,1)} %all-gather.4.cloned.1.call-done, bf16[1,1024,2048]{2,1,0:T(8,128)(2,1)} %param.9), kind=kOutput, calls=%fused_computation.6 | convolution fusion | flops 2147483648 | bytes 8388608 | tf_op jit(solution)/shard_map/td,fd->tf/dot_general | solution.py:35
  274.2 0.0 all-reduce.5.cloned.1.call-update
  275.5 39.4 %psum.31 = f32[]{:T(128)} all-reduce(f32[]{:T(128)S(6)} %add.62), channel_id=1, replica_groups=mesh['layer'=2,'latent'=16] {'layer','latent'}, use_global_device_ids=true, to_apply=%region_8.9 | all-reduce | flops 1 | bytes 8 | tf_op jit(solution)/shard_map/psum | solution.py:49
  315.6 6.7 %fusion.10 = bf16[1,1024,2048]{2,1,0:T(8,128)(2,1)} fusion(f32[1024]{0:T(1024)S(1)} %add_sqrt_fusion, bf16[1,1024,2048]{2,1,0:T(8,128)(2,1)} %param.9, f32[1024]{0:T(1024)S(1)} %broadcast_multiply_fusion, bf16[512,2048]{1,0:T(8,128)(2,1)} %all-gather.4.cloned.1.call-done, bf16[512,1024]{1,0:T(8,128)(2,1)S(1)} %get-tuple-element.8), kind=kOutput, calls=%fused_computation.13 | convolution fusion | flops 2157969408 | bytes 11542528 | tf_op jit(solution)/shard_map/tf,td->fd/dot_general | solution.py:44
  322.2 0.0 all-reduce.5.cloned.1.call-done
  322.2 6.5 %convert_bitcast_fusion = bf16[1,2048,1024]{1,2,0:T(8,128)(2,1)} fusion(bf16[1,512,2048]{2,1,0:T(8,128)(2,1)} %all-gather.6.cloned.1.call-done, f32[512,1024]{1,0:T(8,128)} %all-reduce.5.cloned.1.call-done, s32[512,1024]{1,0:T(8,128)S(1)} %copy-done.1, f32[1024]{0:T(1024)S(1)} %broadcast_multiply_fusion.1), kind=kOutput, calls=%fused_computation.12 | convolution fusion | flops 2151677952 | bytes 10489856 | tf_op jit(solution)/shard_map/td,tf->df/dot_general | solution.py:38
  328.8 6.4 %copy.9 = bf16[1,2048,1024]{2,1,0:T(8,128)(2,1)} copy(bf16[1,2048,1024]{1,2,0:T(8,128)(2,1)} %convert_bitcast_fusion) | data formatting | bytes 8388608
  (3 shorter events, 0.0 us)
Async XLA Ops:
  7.2 66.7 %all-gather.6.cloned.1.call-start = ((), (), s32[]{:S(2)}) async-start(), calls=%async_computation.5 | async-start | bytes 2228224 | tf_op jit(solution)/shard_map/all_gather | solution.py:13
  7.9 92.7 %all-reduce.3.cloned.1.call-start = ((), (), s32[]{:S(2)}) async-start(), calls=%async_computation.1 | async-start | bytes 4194304 | tf_op jit(solution)/shard_map/psum | solution.py:17
  80.4 20.3 %copy-start.1 = (s32[512,1024]{1,0:T(8,128)S(1)}, s32[512,1024]{1,0:T(8,128)}, u32[]{:S(2)}) copy-start(s32[512,1024]{1,0:T(8,128)} %param.11) | copy-start | bytes 6291460
  80.4 20.3 %copy-start.4 = (f32[1024]{0:T(1024)S(1)}, f32[1024]{0:T(1024)}, u32[]{:S(2)}) copy-start(f32[1024]{0:T(1024)} %param.8) | copy-start | bytes 12292
  80.4 124.1 %reduce-scatter.2.cloned.1.call-start = ((), (), s32[]{:S(2)}) async-start(), calls=%async_computation.2 | async-start | bytes 4456448 | tf_op jit(solution)/shard_map/reduce_scatter | solution.py:24
  100.6 2.9 copy-start
  107.9 96.6 %copy-start.2 = (bf16[1,32,2048]{2,1,0:T(8,128)(2,1)S(1)}, bf16[1,32,2048]{2,1,0:T(8,128)(2,1)}, u32[]{:S(2)}) copy-start(bf16[1,32,2048]{2,1,0:T(8,128)(2,1)} %param.6) | copy-start | bytes 393220
  107.9 96.6 %copy-start.3 = (f32[1,2048]{1,0:T(1,128)S(1)}, f32[1,2048]{1,0:T(1,128)}, u32[]{:S(2)}) copy-start(f32[1,2048]{1,0:T(1,128)} %param.10) | copy-start | bytes 24580
  108.0 159.7 %all-gather.4.cloned.1.call-start = ((), (), s32[]{:S(2)}) async-start(), calls=%async_computation.3 | async-start | bytes 2228224 | tf_op jit(solution)/shard_map/all_gather | solution.py:34
  206.8 115.4 %all-reduce.5.cloned.1.call-start = ((), (), s32[]{:S(2)}) async-start(), calls=%async_computation.4 | async-start | bytes 4194304 | tf_op jit(solution)/shard_map/psum | solution.py:36
Sparse Core Ops, SparseCore 0:
  10.7 63.0 all-gather.5
  80.5 20.0 all-reduce.2
  108.1 96.3 reduce-scatter.1
  207.7 59.9 all-gather.3
  274.3 20.1 all-reduce.4
where the time goes:
time: 343 us
  waiting for transfers between devices  238 us (69%)
  blocking collectives  41.9 us (12%)
  matrix products  30.6 us (9%)
  between operations  16.9 us (5%)
  other arithmetic  8.39 us (2%)
  local copies, waits for them, and re-layouts  6.41 us (2%)
    reduce_scatter x1, waiting for transfers between devices, per_device(): lax.psum_scatter(jnp.dot(code_b, decoder, preferred_element_type=jnp.floa...  96.5 us
    all_gather x1, waiting for transfers between devices, per_device(): token_all = lax.all_gather(local_rows, 'latent', axis=0, tiled=True)  65.9 us
    all_gather x1, waiting for transfers between devices, per_device(): lax.all_gather(error_share.astype(jnp.bfloat16), 'latent', axis=0, tiled=...  60.8 us
    psum x1, blocking collectives, per_device(): loss_total = lax.psum(square_part + sparse_part, ('layer', 'latent'))  39.4 us
    psum x1, waiting for transfers between devices, per_device(): preact, norm_sum = lax.psum((layer_pre, row_norm), 'layer')  14.5 us
  transfers between devices with their start and end apart: 5, of which 4 were waited for; matrix products, arithmetic and copies ran while one was open for 3% of the time, Pallas kernels for 0%

commit v1 on v0

--- a/solution.py
+++ b/solution.py
@@ -4,6 +4,7 @@
 from jax.sharding import PartitionSpec as P
 
 sparsity_weight = 0.4
+_deliver_region = lambda view: lax.psum(lax.psum(view, axis_name="layer"), axis_name="latent")
 
 
 def per_device(activations, enc_weight, enc_bias, dec_weight, dec_bias, active_mask):
@@ -46,7 +47,7 @@
     sparse_part = jnp.where(
         layer_index == 0, sparsity_weight * jnp.sum(latent_code * norm_sum), 0.0
     )
-    loss_total = lax.psum(square_part + sparse_part, ("layer", "latent"))
+    loss_total = _deliver_region(square_part + sparse_part)
     loss_value = loss_total / (active_mask.shape[0] * token_all.shape[1])
     return (grad_enc[None], grad_dec[None], loss_value)
 

time: 343 us -> 347 us (1.012)
  blocking collectives: 41.9 us -> 45.7 us
    psum x1 -> x2, blocking collectives: 39.4 us -> 43.2 us  [the longest x1 40.2 us: lax.psum(lax.psum(view, axis_name='layer'), axis_name='latent')]
where the time goes in v1:
time: 347 us
  waiting for transfers between devices  238 us (69%)
  blocking collectives  45.7 us (13%)
  matrix products  30.5 us (9%)
  between operations  16.9 us (5%)
  other arithmetic  8.42 us (2%)
  local copies, waits for them, and re-layouts  6.41 us (2%)
    reduce_scatter x1, waiting for transfers between devices, per_device(): lax.psum_scatter(jnp.dot(code_b, decoder, preferred_element_type=jnp.floa...  96.6 us
    all_gather x1, waiting for transfers between devices, per_device(): token_all = lax.all_gather(local_rows, 'latent', axis=0, tiled=True)  65.9 us
    all_gather x1, waiting for transfers between devices, per_device(): lax.all_gather(error_share.astype(jnp.bfloat16), 'latent', axis=0, tiled=...  60.8 us
    psum x1, blocking collectives, lax.psum(lax.psum(view, axis_name='layer'), axis_name='latent')  40.2 us
    psum x1, waiting for transfers between devices, per_device(): preact, norm_sum = lax.psum((layer_pre, row_norm), 'layer')  14.5 us
  transfers between devices with their start and end apart: 5, of which 4 were waited for; matrix products, arithmetic and copies ran while one was open for 3% of the time, Pallas kernels for 0%

profile of v1, /device:TPU:0, one launch (start us, length us, event | category | flops | bytes accessed | tf_op | source)
XLA Modules:
  0.0 346.6 jit_solution(10385726043062331880)
XLA Ops:
  7.2 0.0 all-gather.6.cloned.1.call-start
  7.2 0.7 all-gather.6.cloned.1.call-update
  7.9 0.0 all-reduce.3.cloned.1.call-start
  7.9 65.9 %all-gather.6.cloned.1.call-done = bf16[1,512,2048]{2,1,0:T(8,128)(2,1)} async-done(((bf16[1,32,2048]{2,1,0:T(8,128)(2,1)}), bf16[1,512,2048]{2,1,0:T(8,128)(2,1)}) %all-gather.6.cloned.1.call-update) | async-done | bytes 2097168 | tf_op jit(solution)/shard_map/all_gather | solution.py:14
  73.9 6.5 %fusion.8 = f32[512,1024]{1,0:T(8,128)} fusion(bf16[1,2048,1024]{2,1,0:T(8,128)(2,1)} %param.7, bf16[1,512,2048]{2,1,0:T(8,128)(2,1)} %all-gather.6.cloned.1.call-done), kind=kOutput, calls=%fused_computation.10 | convolution fusion | flops 2147483648 | bytes 8388608 | tf_op jit(solution)/shard_map/dot_general | solution.py:15
  80.3 0.0 all-reduce.3.cloned.1.call-update
  80.4 0.0 copy-start.1
  80.4 0.0 copy-start.4
  80.4 0.0 reduce-scatter.2.cloned.1.call-start
  80.4 3.2 fusion
  83.7 2.5 psum.37
  86.2 14.5 %all-reduce.3.cloned.1.call-done = f32[512,1024]{1,0:T(8,128)} async-done(((f32[512,1024]{1,0:T(8,128)}), f32[512,1024]{1,0:T(8,128)}) %all-reduce.3.cloned.1.call-update) | async-done | bytes 2097168 | tf_op jit(solution)/shard_map/psum | solution.py:18
  100.6 0.0 copy-done.1
  100.6 0.0 copy-done.4
  100.6 0.0 copy-start
  100.6 2.9 multiply_reduce_fusion
  103.6 0.0 copy-done
  103.6 4.4 %fusion.6 = f32[512,2048]{1,0:T(8,128)} fusion(bf16[1,1024,2048]{2,1,0:T(8,128)(2,1)S(1)} %copy-done, bf16[512,1024]{1,0:T(8,128)(2,1)S(1)} %get-tuple-element.8), kind=kOutput, calls=%fused_computation.8 | convolution fusion | flops 2147483648 | bytes 9437184 | tf_op jit(solution)/shard_map/dot_general | solution.py:26
  107.9 0.0 copy-start.2
  108.0 0.0 copy-start.3
  108.0 0.0 reduce-scatter.2.cloned.1.call-update
  108.0 0.0 all-gather.4.cloned.1.call-start
  108.0 96.6 %reduce-scatter.2.cloned.1.call-done = f32[32,2048]{1,0:T(8,128)} async-done(((f32[512,2048]{1,0:T(8,128)}), f32[32,2048]{1,0:T(8,128)}) %reduce-scatter.2.cloned.1.call-update) | async-done | bytes 262160 | tf_op jit(solution)/shard_map/reduce_scatter | solution.py:25
  204.6 0.0 copy-done.2
  204.6 0.0 copy-done.3
  204.6 2.3 multiply_reduce_fusion.1
  206.9 0.0 all-gather.4.cloned.1.call-update
  206.9 0.0 all-reduce.5.cloned.1.call-start
  206.9 60.8 %all-gather.4.cloned.1.call-done = bf16[512,2048]{1,0:T(8,128)(2,1)} async-done(((bf16[32,2048]{1,0:T(8,128)(2,1)}), bf16[512,2048]{1,0:T(8,128)(2,1)}) %all-gather.4.cloned.1.call-update) | async-done | bytes 2097168 | tf_op jit(solution)/shard_map/all_gather | solution.py:35
  267.7 6.5 %fusion.4 = f32[512,1024]{1,0:T(8,128)} fusion(bf16[512,2048]{1,0:T(8,128)(2,1)} %all-gather.4.cloned.1.call-done, bf16[1,1024,2048]{2,1,0:T(8,128)(2,1)} %param.9), kind=kOutput, calls=%fused_computation.6 | convolution fusion | flops 2147483648 | bytes 8388608 | tf_op jit(solution)/shard_map/td,fd->tf/dot_general | solution.py:36
  274.2 0.0 all-reduce.5.cloned.1.call-update
  275.5 3.0 psum.38
  278.5 40.2 %psum.39 = f32[]{:T(128)} all-reduce(f32[]{:T(128)} %psum.38), channel_id=1, replica_groups=mesh['layer'=2,'latent'=16] {'latent'}, use_global_device_ids=true, to_apply=%region_9.10 | all-reduce | flops 1 | bytes 8 | tf_op jit(solution)/shard_map/psum | solution.py:7
  319.3 6.7 %fusion.10 = bf16[1,1024,2048]{2,1,0:T(8,128)(2,1)} fusion(f32[1024]{0:T(1024)S(1)} %add_sqrt_fusion, bf16[1,1024,2048]{2,1,0:T(8,128)(2,1)} %param.9, f32[1024]{0:T(1024)S(1)} %broadcast_multiply_fusion, bf16[512,2048]{1,0:T(8,128)(2,1)} %all-gather.4.cloned.1.call-done, bf16[512,1024]{1,0:T(8,128)(2,1)S(1)} %get-tuple-element.8), kind=kOutput, calls=%fused_computation.13 | convolution fusion | flops 2157969408 | bytes 11542528 | tf_op jit(solution)/shard_map/tf,td->fd/dot_general | solution.py:45
  326.0 0.0 all-reduce.5.cloned.1.call-done
  326.0 6.5 %convert_bitcast_fusion = bf16[1,2048,1024]{1,2,0:T(8,128)(2,1)} fusion(bf16[1,512,2048]{2,1,0:T(8,128)(2,1)} %all-gather.6.cloned.1.call-done, f32[512,1024]{1,0:T(8,128)} %all-reduce.5.cloned.1.call-done, s32[512,1024]{1,0:T(8,128)S(1)} %copy-done.1, f32[1024]{0:T(1024)S(1)} %broadcast_multiply_fusion.1), kind=kOutput, calls=%fused_computation.12 | convolution fusion | flops 2151677952 | bytes 10489856 | tf_op jit(solution)/shard_map/td,tf->df/dot_general | solution.py:39
  332.6 6.4 %copy.9 = bf16[1,2048,1024]{2,1,0:T(8,128)(2,1)} copy(bf16[1,2048,1024]{1,2,0:T(8,128)(2,1)} %convert_bitcast_fusion) | data formatting | bytes 8388608
  (3 shorter events, 0.0 us)
Async XLA Ops:
  7.2 66.7 %all-gather.6.cloned.1.call-start = ((), (), s32[]{:S(2)}) async-start(), calls=%async_computation.5 | async-start | bytes 2228224 | tf_op jit(solution)/shard_map/all_gather | solution.py:14
  7.9 92.7 %all-reduce.3.cloned.1.call-start = ((), (), s32[]{:S(2)}) async-start(), calls=%async_computation.1 | async-start | bytes 4194304 | tf_op jit(solution)/shard_map/psum | solution.py:18
  80.4 20.3 %copy-start.1 = (s32[512,1024]{1,0:T(8,128)S(1)}, s32[512,1024]{1,0:T(8,128)}, u32[]{:S(2)}) copy-start(s32[512,1024]{1,0:T(8,128)} %param.11) | copy-start | bytes 6291460
  80.4 20.3 %copy-start.4 = (f32[1024]{0:T(1024)S(1)}, f32[1024]{0:T(1024)}, u32[]{:S(2)}) copy-start(f32[1024]{0:T(1024)} %param.8) | copy-start | bytes 12292
  80.4 124.2 %reduce-scatter.2.cloned.1.call-start = ((), (), s32[]{:S(2)}) async-start(), calls=%async_computation.2 | async-start | bytes 4456448 | tf_op jit(solution)/shard_map/reduce_scatter | solution.py:25
  100.6 2.9 copy-start
  107.9 96.6 %copy-start.2 = (bf16[1,32,2048]{2,1,0:T(8,128)(2,1)S(1)}, bf16[1,32,2048]{2,1,0:T(8,128)(2,1)}, u32[]{:S(2)}) copy-start(bf16[1,32,2048]{2,1,0:T(8,128)(2,1)} %param.6) | copy-start | bytes 393220
  108.0 96.6 %copy-start.3 = (f32[1,2048]{1,0:T(1,128)S(1)}, f32[1,2048]{1,0:T(1,128)}, u32[]{:S(2)}) copy-start(f32[1,2048]{1,0:T(1,128)} %param.10) | copy-start | bytes 24580
  108.0 159.7 %all-gather.4.cloned.1.call-start = ((), (), s32[]{:S(2)}) async-start(), calls=%async_computation.3 | async-start | bytes 2228224 | tf_op jit(solution)/shard_map/all_gather | solution.py:35
  206.9 119.1 %all-reduce.5.cloned.1.call-start = ((), (), s32[]{:S(2)}) async-start(), calls=%async_computation.4 | async-start | bytes 4194304 | tf_op jit(solution)/shard_map/psum | solution.py:37
Sparse Core Ops, SparseCore 0:
  10.7 63.0 all-gather.5
  80.5 20.0 all-reduce.2
  108.1 96.4 reduce-scatter.1
  207.8 59.8 all-gather.3
  274.4 20.0 all-reduce.4
